TPU v7x, 32 devices: a whole 2x2x4 slice. The times are simulated.
32 devices in a mesh: mode: 8 (over y, x, core), rows: 4 (over z).
Axes of the slice: x: 2, y: 2, z: 4, core: 2. Of those that a mesh axis runs over, the one named last changes fastest.
Arguments:
- tangents: float32 [128, 3, 32, 1024], P('mode', None, 'rows'), may hold values from -6 to 6
- checkpoints: float32 [8, 3, 32, 1024], P(None, None, 'rows', 'mode'), may hold values from 0 to 0.5
- owner_order: int32 [8], replicated, may hold values from 0 to 7, each once
- land_mask: int32 [32, 1024], P('rows'), may hold values 0 or 1
- coefficients: float32 [128, 128], replicated, may hold values from -0.9 to 0.9
Outputs:
- vectors: float32 [128, 3, 32, 1024], P(None, None, 'rows', 'mode')
Inputs may be any that keep to these rules, and one draw needn't show every extreme that they name: `owner_order`: every checkpoint slot is named by exactly one step.
All inputs are finite; a program needn't handle non-finite values. No bound on the sum of `land_mask` on one device may be relied on, other than what follows from the above.
Results may differ from a plain program's by a relative error of at most 0.0002.
Values sent between devices are 32-bit elements; how exact they have to be, the bound alone decides.
A program may use at most 64 MiB of HBM per device.

v0:
```python
import functools

import jax
import jax.numpy as jnp
from jax import lax
from jax.experimental import pallas as pl
from jax.experimental.pallas import tpu as pltpu
from jax.sharding import PartitionSpec as P

mean_depth = 1.0
gravity = 1.0
coriolis = 0.5
time_step = 0.5


def padded(cells, sides, width):
    for axis, dim in sides:
        count = lax.axis_size(axis)
        ends = count - 1
        head = lax.slice_in_dim(cells, 0, width, axis=dim)
        tail = lax.slice_in_dim(cells, cells.shape[dim] - width, cells.shape[dim], axis=dim)
        cells = jnp.concatenate(
            [
                lax.ppermute(tail, axis, [(i, (i + 1) % count) for i in range(ends)]),
                cells,
                lax.ppermute(head, axis, [((i + 1) % count, i) for i in range(ends)]),
            ],
            axis=dim,
        )
    return cells


def deriv_x(values):
    return 0.5 * (jnp.roll(values, -1, -1) - jnp.roll(values, 1, -1))


def deriv_y(values):
    return 0.5 * (values[..., 2:, :] - values[..., :-2, :])


def interior(values):
    return values[..., 1:-1, :]


def tendency(base_flow, current):
    depth_total = mean_depth + base_flow[0]
    flow_u = base_flow[1]
    flow_v = base_flow[2]
    height = current[:, 0]
    zonal = current[:, 1]
    meridional = current[:, 2]
    flux_x = depth_total * zonal + height * flow_u
    flux_y = depth_total * meridional + height * flow_v
    height_rate = -(interior(deriv_x(flux_x)) + deriv_y(flux_y))
    zonal_mid = interior(zonal)
    merid_mid = interior(meridional)
    flow_umid = interior(flow_u)
    flow_vmid = interior(flow_v)
    zonal_rate = (
        -(
            flow_umid * interior(deriv_x(zonal))
            + zonal_mid * interior(deriv_x(flow_u))
            + flow_vmid * deriv_y(zonal)
            + merid_mid * deriv_y(flow_u)
        )
        + coriolis * merid_mid
        - gravity * interior(deriv_x(height))
    )
    merid_rate = (
        -(
            flow_umid * interior(deriv_x(meridional))
            + zonal_mid * interior(deriv_x(flow_v))
            + flow_vmid * deriv_y(meridional)
            + merid_mid * deriv_y(flow_v)
        )
        - coriolis * zonal_mid
        - gravity * deriv_y(height)
    )
    return jnp.stack([height_rate, zonal_rate, merid_rate], 1)


def step_wide(base_wide, state_wide, wet_wide):
    slope_one = tendency(base_wide, state_wide)
    middle = wet_wide[1:-1] * (state_wide[:, :, 1:-1] + time_step * slope_one)
    slope_two = tendency(base_wide[:, 1:-1], middle)
    return wet_wide[2:-2] * (
        state_wide[:, :, 2:-2] + 0.5 * time_step * (slope_one[:, :, 1:-1] + slope_two)
    )


def on_device_general(tangents, checkpoints, owner_order, land_mask, coefficients):
    wet_mask = land_mask.astype(jnp.float32)
    current = wet_mask * tangents
    depth = 2
    flows_wide, wet_stack = (
        padded(checkpoints, (("rows", 2),), depth),
        padded(wet_mask[None, None], (("rows", 2),), depth),
    )
    wet_wide = wet_stack[0, 0]

    def fetch_flow(step_index):
        held_tile = lax.dynamic_index_in_dim(flows_wide, owner_order[step_index], 0, keepdims=False)
        return lax.all_gather(held_tile, "mode", axis=2, tiled=True)

    total_steps = owner_order.shape[0]

    def advance(step_index, current):
        widened = padded(current, (("rows", 2),), 2)
        return step_wide(fetch_flow(step_index), widened, wet_wide)

    final = lax.fori_loop(0, total_steps, advance, current)
    mixing = jnp.eye(coefficients.shape[0], dtype=jnp.float32) + jnp.triu(coefficients)
    cell_block = lax.all_to_all(final, "mode", split_axis=3, concat_axis=0, tiled=True)
    flattened = cell_block.reshape(cell_block.shape[0], -1)
    mixed = jnp.dot(
        mixing.T, flattened, precision=lax.Precision.HIGHEST, preferred_element_type=jnp.float32
    )
    return mixed.reshape(cell_block.shape)


LANES = 128
SUB = 8
COEFS = 7


def tile_shift(values, lane, ahead):
    tiles = values.shape[0]
    if ahead:
        rolled = pltpu.roll(values, LANES - 1, 2)
        beside = jnp.concatenate([rolled[1:], rolled[:1]], axis=0) if tiles > 1 else rolled
        return jnp.where(lane == LANES - 1, beside, rolled)
    rolled = pltpu.roll(values, 1, 2)
    beside = jnp.concatenate([rolled[-1:], rolled[:-1]], axis=0) if tiles > 1 else rolled
    return jnp.where(lane == 0, beside, rolled)


def diff_x(values, lane):
    return tile_shift(values, lane, True) - tile_shift(values, lane, False)


def zero_pads(ref, strips):
    lead = ref.shape[:-2]
    edge = jnp.zeros(lead + (SUB, LANES), jnp.float32)
    ref[..., pl.ds(0, SUB), :] = edge
    ref[..., pl.ds(SUB * (strips + 1), SUB), :] = edge


def band(strip, shift=0):
    return pl.ds(SUB * (strip + 1) + shift, SUB)


def build_coefs(order, base_ref, coef, flow_pad, strips, steps, lane):
    zero_pads(flow_pad, strips)

    def one(step, carry):
        first = 3 * order[step]
        for strip in range(strips):
            coef[step, 0, :, pl.ds(SUB * strip, SUB), :] = 0.0625 * (
                mean_depth + base_ref[:, strip, first]
            )
            flow_pad[0, :, band(strip), :] = 0.25 * base_ref[:, strip, first + 1]
            flow_pad[1, :, band(strip), :] = 0.25 * base_ref[:, strip, first + 2]
        for strip in range(strips):
            rows = pl.ds(SUB * strip, SUB)
            flow_u = flow_pad[0, :, band(strip), :]
            flow_v = flow_pad[1, :, band(strip), :]
            coef[step, 1, :, rows, :] = flow_u
            coef[step, 2, :, rows, :] = flow_v
            coef[step, 3, :, rows, :] = diff_x(flow_u, lane)
            coef[step, 4, :, rows, :] = 0.25 - (
                flow_pad[0, :, band(strip, 1), :] - flow_pad[0, :, band(strip, -1), :]
            )
            coef[step, 5, :, rows, :] = 0.25 + diff_x(flow_v, lane)
            coef[step, 6, :, rows, :] = (
                flow_pad[1, :, band(strip, 1), :] - flow_pad[1, :, band(strip, -1), :]
            )
        return carry

    lax.fori_loop(0, steps, one, 0)


def store_flux(source, flux, coef, step, strip):
    rows = pl.ds(SUB * strip, SUB)
    flux[:, band(strip), :] = (
        coef[step, 0, :, rows, :] * source[2, :, band(strip), :]
        + coef[step, 2, :, rows, :] * source[0, :, band(strip), :]
    )


def scaled_rates(source, flux, coef, step, strip, lane):
    rows = pl.ds(SUB * strip, SUB)
    here, above, below = band(strip), band(strip, 1), band(strip, -1)
    height, zonal, merid = source[0, :, here, :], source[1, :, here, :], source[2, :, here, :]
    depth, flow_u, flow_v, du_dx, turn_v, turn_u, dv_dy = (
        coef[step, i, :, rows, :] for i in range(COEFS)
    )
    flux_x = depth * zonal + flow_u * height
    rate_h = diff_x(flux_x, lane) + (flux[:, above, :] - flux[:, below, :])
    rate_u = turn_v * merid - (
        flow_u * diff_x(zonal, lane)
        + du_dx * zonal
        + flow_v * (source[1, :, above, :] - source[1, :, below, :])
        + diff_x(height, lane)
    )
    rate_v = (
        flow_u * diff_x(merid, lane)
        + turn_u * zonal
        + flow_v * (source[2, :, above, :] - source[2, :, below, :])
        + dv_dy * merid
        + (source[0, :, above, :] - source[0, :, below, :])
    )
    return (height, zonal, merid), (-rate_h, rate_u, -rate_v)


def run_steps(state, middle, flux, coef, wet, strips, steps, lane):
    def one(step, carry):
        for strip in range(strips):
            store_flux(state, flux, coef, step, strip)
        for strip in range(strips):
            held, rates = scaled_rates(state, flux, coef, step, strip, lane)
            water = wet[:, pl.ds(SUB * strip, SUB), :]
            for f in range(3):
                middle[f, :, band(strip), :] = water * (held[f] + rates[f])
        for strip in range(strips):
            store_flux(middle, flux, coef, step, strip)
        for strip in range(strips):
            held, rates = scaled_rates(middle, flux, coef, step, strip, lane)
            water = wet[:, pl.ds(SUB * strip, SUB), :]
            for f in range(3):
                state[f, :, band(strip), :] = state[f, :, band(strip), :] + water * (
                    held[f] + rates[f]
                )
        return carry

    lax.fori_loop(0, steps, one, 0)


def steps_kernel(strips, tiles, steps, kept, order_ref, base_ref, land_ref, tan_ref, out_ref,
                 base_all, whole, leaving, coef, wet, state, middle, flux, flow_pad,
                 z_send, z_recv, x_send, x_recv, p_send, p_recv,
                 in_send, in_recv, out_send, out_recv, known, land, order, fetch):
    m = lax.axis_index("mode")
    r = lax.axis_index("rows")
    everyone = tiles * strips
    me = m * strips + r
    chips = tiles // 2
    pairs = 2 * (m // 2)
    core = m - pairs
    partner = pairs + 1 - core
    mask_at = 3 * steps
    lane = lax.broadcasted_iota(jnp.int32, (tiles, SUB, LANES), 2)

    def other_chip(j):
        return lax.rem(m + 2 * j, tiles)

    def send(source, target, sent, received, mode, row):
        pltpu.make_async_remote_copy(
            src_ref=source, dst_ref=target, send_sem=sent, recv_sem=received,
            device_id=(mode, row), device_id_type=pl.DeviceIdType.MESH,
        ).start()

    def drain(ref, sem):
        pltpu.make_async_copy(ref, ref, sem).wait()

    barrier = pltpu.get_barrier_semaphore()

    def signal(sem, mode, row):
        pl.semaphore_signal(
            sem, inc=1, device_id=(mode, row), device_id_type=pl.DeviceIdType.MESH
        )

    for j in range(1, strips):
        signal(barrier, m, lax.rem(r + j, strips))
    for j in range(1, tiles):
        signal(barrier, lax.rem(m + j, tiles), r)

    own = base_all.at[m, r]
    tile_of_land = land_ref.at[:, pl.ds(pl.multiple_of(m * LANES, LANES), LANES)]
    fetch_base = pltpu.make_async_copy(base_ref, own.at[pl.ds(0, mask_at)], fetch.at[0])
    fetch_land = pltpu.make_async_copy(tile_of_land, land, fetch.at[1])
    fetch_order = pltpu.make_async_copy(order_ref, order, fetch.at[2])
    fetch_base.start()
    fetch_land.start()
    fetch_order.start()
    fetch_land.wait()
    own[mask_at] = land[...].astype(jnp.float32)
    fetch_base.wait()
    fetch_order.wait()

    pl.semaphore_wait(barrier, strips + tiles - 2)

    def send_in(k, j):
        q = lax.rem(r + j, strips)
        send(tan_ref.at[q * kept + k], whole.at[k, r], in_send, in_recv.at[k], m, q)

    def relay(q):
        strip = base_all.at[m, q]

        @pl.when(jnp.logical_and(q <= r, r < strips - 1))
        def _():
            send(strip, strip, z_send.at[0, q], z_recv.at[q], m, r + 1)

        @pl.when(jnp.logical_and(q >= r, r > 0))
        def _():
            send(strip, strip, z_send.at[1, q], z_recv.at[q], m, r - 1)

        for j in range(1, chips):
            send(strip, strip, x_send, x_recv.at[m], other_chip(j), r)

    relay(r)
    for j in range(1, strips):
        send_in(0, j)

        @pl.when(r >= j)
        def _():
            drain(base_all.at[m, r - j], z_recv.at[r - j])
            relay(r - j)

        @pl.when(r + j < strips)
        def _():
            drain(base_all.at[m, r + j], z_recv.at[r + j])
            relay(r + j)

    for k in range(kept):
        if k > 0:
            for j in range(1, strips):
                send_in(k, j)
        pltpu.make_async_copy(tan_ref.at[r * kept + k], whole.at[k, r], in_recv.at[k]).start()
    for j in range(1, tiles):
        signal(known, lax.rem(m + j, tiles), r)
    send(base_all.at[m], base_all.at[m], p_send, p_recv, partner, r)
    for ref in (state, middle, flux):
        zero_pads(ref, strips)
    for j in range(1, chips):
        tile = other_chip(j)
        drain(base_all.at[tile], x_recv.at[tile])
        send(base_all.at[tile], base_all.at[tile], p_send, p_recv, partner, r)
    drain(base_all.at[pl.ds(0, chips)], p_recv)

    for strip in range(strips):
        wet[:, pl.ds(SUB * strip, SUB), :] = base_all[:, strip, mask_at]
    build_coefs(order, base_all, coef, flow_pad, strips, steps, lane)

    def one_mode(k, carry):
        drain(whole.at[k], in_recv.at[k])
        for f, scale in enumerate((0.25, 1.0, 1.0)):
            for strip in range(strips):
                for t in range(tiles):
                    state[f, t, band(strip), :] = (
                        scale * wet[t, pl.ds(SUB * strip, SUB), :]
                    ) * whole[k, strip, f, :, pl.ds(LANES * t, LANES)]
        run_steps(state, middle, flux, coef, wet, strips, steps, lane)
        down = 0.5 ** steps
        for f, scale in enumerate((4.0 * down, down, down)):
            for strip in range(strips):
                for t in range(tiles):
                    leaving[k, t * strips + strip, f] = scale * state[f, t, band(strip), :]

        def post(row):
            def to(j, carry):
                mode = lax.rem(m + j, tiles)
                send(leaving.at[k, mode * strips + row], out_ref.at[me, k], out_send, out_recv,
                     mode, row)
                return carry

            return to

        for j in range(strips):
            row = lax.rem(r + strips // 2 + j, strips)
            lax.fori_loop(1 if j == strips - strips // 2 else 0, tiles, post(row), 0)
        pltpu.make_async_copy(leaving.at[k, me], out_ref.at[me, k], out_recv).start()
        return carry

    pl.semaphore_wait(known, tiles - 1)
    lax.fori_loop(0, kept, one_mode, 0)

    for q in range(strips):

        @pl.when(jnp.logical_and(q <= r, r < strips - 1))
        def _():
            drain(base_all.at[m, q], z_send.at[0, q])

        @pl.when(jnp.logical_and(q >= r, r > 0))
        def _():
            drain(base_all.at[m, q], z_send.at[1, q])

    drain(base_all.at[pl.ds(0, chips - 1)], x_send)
    drain(base_all.at[pl.ds(0, chips)], p_send)
    drain(whole.at[:, pl.ds(0, strips - 1)], in_send)
    drain(leaving.at[:, pl.ds(0, everyone - 1)], out_send)
    drain(out_ref, out_recv)


def step_modes(order, base, land, tangents):
    strips, tiles = lax.axis_size("rows"), lax.axis_size("mode")
    held, fields, rows, columns = tangents.shape
    steps = base.shape[0]
    kept = held // strips
    everyone = tiles * strips
    tall = SUB * (strips + 2)
    hbm = pl.BlockSpec(memory_space=pltpu.HBM)
    operands = (order, base.reshape(steps * fields, rows, LANES), land, tangents)
    dma = pltpu.SemaphoreType.DMA
    return pl.pallas_call(
        functools.partial(steps_kernel, strips, tiles, steps, kept),
        out_shape=jax.ShapeDtypeStruct((everyone, kept, fields, rows, LANES), jnp.float32),
        in_specs=[hbm] * 4,
        out_specs=pl.BlockSpec(memory_space=pl.ANY),
        scratch_shapes=[
            pltpu.VMEM((tiles, strips, steps * fields + 1, rows, LANES), jnp.float32),
            pltpu.VMEM((kept, strips, fields, rows, columns), jnp.float32),
            pltpu.VMEM((kept, everyone, fields, rows, LANES), jnp.float32),
            pltpu.VMEM((steps, COEFS, tiles, SUB * strips, LANES), jnp.float32),
            pltpu.VMEM((tiles, SUB * strips, LANES), jnp.float32),
            pltpu.VMEM((3, tiles, tall, LANES), jnp.float32),
            pltpu.VMEM((3, tiles, tall, LANES), jnp.float32),
            pltpu.VMEM((tiles, tall, LANES), jnp.float32),
            pltpu.VMEM((2, tiles, tall, LANES), jnp.float32),
            dma((2, strips)), dma((strips,)), dma, dma((tiles,)), dma, dma,
            dma, dma((kept,)), dma, dma, pltpu.SemaphoreType.REGULAR,
            pltpu.VMEM((rows, LANES), jnp.int32), pltpu.SMEM((steps,), jnp.int32), dma((3,)),
        ],
        compiler_params=pltpu.CompilerParams(
            collective_id=0, has_side_effects=True, vmem_limit_bytes=24 << 20
        ),
    )(*(pltpu.with_memory_space_constraint(held_in_hbm, pltpu.HBM) for held_in_hbm in operands))


def halves(values):
    high = values.astype(jnp.bfloat16)
    return high, (values - high.astype(jnp.float32)).astype(jnp.bfloat16)


def mix_kernel(coef_ref, cells_ref, out_ref, staged, sems):
    modes, spots, _ = cells_ref.shape
    row = lax.broadcasted_iota(jnp.int32, (modes, modes), 0)
    col = lax.broadcasted_iota(jnp.int32, (modes, modes), 1)
    mixing = jnp.where(row <= col, coef_ref[...], 0.0) + jnp.where(row == col, 1.0, 0.0)
    high, low = halves(mixing.T)
    turned = jnp.concatenate(
        [jnp.concatenate([high, high], 1), jnp.concatenate([low, low], 1)], 0
    )
    cells = cells_ref.reshape(modes * spots, LANES)
    copies = []
    for group in range(spots // SUB):
        out = staged.at[group].reshape(modes * SUB, LANES)
        for spot in range(0, SUB, 2):
            first = SUB * group + spot
            high, low = halves(jnp.concatenate(
                [cells[pl.ds(first + i, modes, stride=spots), :] for i in (0, 1)], 1
            ))
            mixed = jnp.dot(
                turned, jnp.concatenate([high, low], 0), preferred_element_type=jnp.float32
            )
            mixed = mixed[:modes] + mixed[modes:]
            for i in (0, 1):
                out[pl.ds(spot + i, modes, stride=SUB), :] = mixed[:, LANES * i:LANES * (i + 1)]
        copies.append(pltpu.make_async_copy(
            staged.at[group], out_ref.at[:, pl.ds(SUB * group, SUB)], sems.at[group]
        ))
        copies[-1].start()
    for copy in copies:
        copy.wait()


def mix(coefficients, cells):
    modes, spots, _ = cells.shape
    return pl.pallas_call(
        mix_kernel,
        out_shape=jax.ShapeDtypeStruct(cells.shape, jnp.float32),
        in_specs=[pl.BlockSpec(memory_space=pltpu.VMEM)] * 2,
        out_specs=pl.BlockSpec(memory_space=pltpu.HBM),
        scratch_shapes=[
            pltpu.VMEM((spots // SUB, modes, SUB, LANES), jnp.float32),
            pltpu.SemaphoreType.DMA((spots // SUB,)),
        ],
        compiler_params=pltpu.CompilerParams(vmem_limit_bytes=8 << 20),
    )(coefficients, cells)


def on_device_whole(tangents, checkpoints, owner_order, land_mask, coefficients):
    fields, rows = tangents.shape[1:3]
    placed = step_modes(owner_order, checkpoints, land_mask, tangents)
    mixed = mix(coefficients, placed.reshape(coefficients.shape[0], fields * rows, LANES))
    return mixed.reshape(coefficients.shape[0], fields, rows, LANES)


def on_device(tangents, checkpoints, owner_order, land_mask, coefficients):
    strips = lax.axis_size("rows")
    held, _, rows, columns = tangents.shape
    fits = (
        held % strips == 0 and strips > 1 and lax.axis_size("mode") % 2 == 0
        and lax.axis_size("mode") > 2 and rows == SUB and checkpoints.shape[-1] == LANES and strips <= 8
        and coefficients.shape[0] % LANES == 0
    )
    chosen = on_device_whole if fits else on_device_general
    return chosen(tangents, checkpoints, owner_order, land_mask, coefficients)


def solution(mesh):
    placed = (
        P("mode", None, "rows", None),
        P(None, None, "rows", "mode"),
        P(),
        P("rows", None),
        P(),
    )
    return jax.shard_map(
        on_device,
        mesh=mesh,
        in_specs=placed,
        out_specs=P(None, None, "rows", "mode"),
        check_vma=False,
    )
```

profile of v0, /device:TPU:0, one launch (start us, length us, event | category | flops | bytes accessed | tf_op | source)
XLA Modules:
  0.0 80.6 jit_solution(11525861423642117754)
XLA Ops:
  0.0 0.0 copy-start
  0.0 79.0 %shard_map.55 = f32[32,4,3,8,128]{4,3,2,1,0:T(8,128)S(1)} custom-call(s32[8]{0:T(128)} %order_ref.1, f32[24,8,128]{2,1,0:T(8,128)} %bitcast.4, s32[8,1024]{1,0:T(8,128)} %land_ref.1, f32[16,3,8,1024]{3,2,1,0:T(8,128)} %tan_ref.1), custom_call_target="tpu_custom_call" | custom-call | tf_op jit(solution)/shard_map/pallas_call | solution.py:404
  79.0 0.0 copy-done
  79.0 1.6 %shard_map.56 = f32[128,24,128]{2,1,0:T(8,128)} custom-call(f32[128,128]{1,0:T(8,128)S(1)} %copy-done, f32[128,24,128]{2,1,0:T(8,128)S(1)} %bitcast.3), custom_call_target="tpu_custom_call" | custom-call | tf_op jit(solution)/shard_map/pallas_call | solution.py:468
Async XLA Ops:
  0.0 79.0 %copy-start = (f32[128,128]{1,0:T(8,128)S(1)}, f32[128,128]{1,0:T(8,128)}, u32[]{:S(2)}) copy-start(f32[128,128]{1,0:T(8,128)} %coef_ref.1) | copy-start | bytes 196612
where the time goes:
time: 80.8 us; the launch traced here: 80.6 us
  Pallas kernels  80.6 us (100%)
    pallas_call x1, Pallas kernels, step_modes(): pl.pallas_call(functools.partial(steps_kernel, strips, tiles, steps, kept...  79 us

commit v1 on v0

--- a/solution.py
+++ b/solution.py
@@ -238,7 +238,8 @@
 def steps_kernel(strips, tiles, steps, kept, order_ref, base_ref, land_ref, tan_ref, out_ref,
                  base_all, whole, leaving, coef, wet, state, middle, flux, flow_pad,
                  z_send, z_recv, x_send, x_recv, p_send, p_recv,
-                 in_send, in_recv, out_send, out_recv, known, land, order, fetch):
+                 in_send, in_recv, out_send, out_recv, line, plane, half_in, cross,
+                 land, order, fetch):
     m = lax.axis_index("mode")
     r = lax.axis_index("rows")
     everyone = tiles * strips
@@ -263,53 +264,176 @@
         pltpu.make_async_copy(ref, ref, sem).wait()
 
     barrier = pltpu.get_barrier_semaphore()
+    half = strips // 2
+    upper = r >= half
+    at_end = jnp.logical_or(r == 0, r == strips - 1)
+    at_mid = jnp.logical_or(r == half - 1, r == half)
+    not_end, not_mid = jnp.logical_not(at_end), jnp.logical_not(at_mid)
+    inner = jnp.where(upper, r - 1, r + 1)
+    outer = jnp.where(upper, r + 1, r - 1)
 
     def signal(sem, mode, row):
         pl.semaphore_signal(
             sem, inc=1, device_id=(mode, row), device_id_type=pl.DeviceIdType.MESH
         )
 
-    for j in range(1, strips):
-        signal(barrier, m, lax.rem(r + j, strips))
-    for j in range(1, tiles):
-        signal(barrier, lax.rem(m + j, tiles), r)
+    def signal_plane(sem):
+        for j in range(1, tiles):
+            signal(sem, lax.rem(m + j, tiles), r)
+
+    def sibling(i):
+        return jnp.where(upper, half + lax.rem(r + i, half), lax.rem(r + i, half))
+
+    def opposite(i):
+        return jnp.where(upper, half - 1 - i, half + i)
+
+    @pl.when(at_mid)
+    def _():
+        signal(barrier, m, inner)
+
+    @pl.when(jnp.logical_and(at_mid, not_end))
+    def _():
+        signal(barrier, m, outer)
+
+    @pl.when(at_end)
+    def _():
+        signal_plane(barrier)
 
     own = base_all.at[m, r]
     tile_of_land = land_ref.at[:, pl.ds(pl.multiple_of(m * LANES, LANES), LANES)]
     fetch_base = pltpu.make_async_copy(base_ref, own.at[pl.ds(0, mask_at)], fetch.at[0])
     fetch_land = pltpu.make_async_copy(tile_of_land, land, fetch.at[1])
     fetch_order = pltpu.make_async_copy(order_ref, order, fetch.at[2])
+    fetch_land.start()
     fetch_base.start()
-    fetch_land.start()
     fetch_order.start()
+
+    @pl.when(at_end)
+    def _():
+        pl.semaphore_wait(barrier, tiles)
+
+    @pl.when(not_end)
+    def _():
+        pl.semaphore_wait(barrier, 1)
+
+    if half > 2:
+
+        @pl.when(jnp.logical_and(not_end, not_mid))
+        def _():
+            signal(barrier, m, outer)
+
+    def send_in(k, q):
+        send(tan_ref.at[q * kept + k], whole.at[k, r], in_send, in_recv.at[k], m, q)
+
+    def pass_up(q):
+        strip = base_all.at[m, q]
+        send(strip, strip, z_send.at[0, q], z_recv.at[q], m, r + 1)
+
+    def pass_down(q):
+        strip = base_all.at[m, q]
+        send(strip, strip, z_send.at[1, q], z_recv.at[q], m, r - 1)
+
+    def spread(q):
+        strip = base_all.at[m, q]
+        for j in range(1, chips):
+            send(strip, strip, x_send, x_recv.at[m], other_chip(j), r)
+
+    early = min(2, kept)
+    lead = 2
+    send_in(0, inner)
     fetch_land.wait()
     own[mask_at] = land[...].astype(jnp.float32)
     fetch_base.wait()
     fetch_order.wait()
 
-    pl.semaphore_wait(barrier, strips + tiles - 2)
-
-    def send_in(k, j):
-        q = lax.rem(r + j, strips)
-        send(tan_ref.at[q * kept + k], whole.at[k, r], in_send, in_recv.at[k], m, q)
+    @pl.when(upper)
+    def _():
+        pass_down(r)
+
+    @pl.when(jnp.logical_not(upper))
+    def _():
+        pass_up(r)
+
+    for k in range(1, early):
+        send_in(k, inner)
+
+    @pl.when(not_mid)
+    def _():
+        signal(line, m, inner)
+
+    @pl.when(at_end)
+    def _():
+        signal_plane(plane)
+        spread(r)
+
+    @pl.when(not_end)
+    def _():
+        pl.semaphore_wait(line, 1)
+
+        @pl.when(upper)
+        def _():
+            pass_up(r)
+
+        @pl.when(jnp.logical_not(upper))
+        def _():
+            pass_down(r)
+
+        send_in(0, outer)
+
+    @pl.when(at_end)
+    def _():
+        pl.semaphore_wait(plane, tiles - 1)
+        for i in range(1, half):
+            signal(half_in, m, sibling(i))
+
+    @pl.when(not_end)
+    def _():
+        pl.semaphore_wait(half_in, 1)
+        spread(r)
+
+    @pl.when(at_mid)
+    def _():
+        signal(cross, m, inner)
+        pl.semaphore_wait(cross, 1)
+        for i in range(1, half):
+            signal(cross, m, sibling(i))
+
+    def send_rest(k):
+        for i in range(half):
+            q = opposite(i)
+            if k < early:
+
+                @pl.when(q != inner)
+                def _():
+                    send_in(k, q)
+            else:
+                send_in(k, q)
+        for i in range(1, half):
+            q = sibling(i)
+            if k < early:
+                done = q == inner
+                if k == 0:
+                    done = jnp.logical_or(done, q == outer)
+
+                @pl.when(jnp.logical_not(done))
+                def _():
+                    send_in(k, q)
+            else:
+                send_in(k, q)
 
     def relay(q):
-        strip = base_all.at[m, q]
-
-        @pl.when(jnp.logical_and(q <= r, r < strips - 1))
-        def _():
-            send(strip, strip, z_send.at[0, q], z_recv.at[q], m, r + 1)
-
-        @pl.when(jnp.logical_and(q >= r, r > 0))
-        def _():
-            send(strip, strip, z_send.at[1, q], z_recv.at[q], m, r - 1)
-
-        for j in range(1, chips):
-            send(strip, strip, x_send, x_recv.at[m], other_chip(j), r)
-
-    relay(r)
+
+        @pl.when(jnp.logical_and(q < r, r < strips - 1))
+        def _():
+            pass_up(q)
+
+        @pl.when(jnp.logical_and(q > r, r > 0))
+        def _():
+            pass_down(q)
+
+        spread(q)
+
     for j in range(1, strips):
-        send_in(0, j)
 
         @pl.when(r >= j)
         def _():
@@ -321,13 +445,18 @@
             drain(base_all.at[m, r + j], z_recv.at[r + j])
             relay(r + j)
 
+        if j == 1:
+
+            @pl.when(not_mid)
+            def _():
+                pl.semaphore_wait(cross, 1)
+
+            send_rest(0)
+
     for k in range(kept):
         if k > 0:
-            for j in range(1, strips):
-                send_in(k, j)
+            send_rest(k)
         pltpu.make_async_copy(tan_ref.at[r * kept + k], whole.at[k, r], in_recv.at[k]).start()
-    for j in range(1, tiles):
-        signal(known, lax.rem(m + j, tiles), r)
     send(base_all.at[m], base_all.at[m], p_send, p_recv, partner, r)
     for ref in (state, middle, flux):
         zero_pads(ref, strips)
@@ -356,22 +485,37 @@
                 for t in range(tiles):
                     leaving[k, t * strips + strip, f] = scale * state[f, t, band(strip), :]
 
-        def post(row):
+        def post(row, mode):
+            send(leaving.at[k, mode * strips + row], out_ref.at[me, k], out_send, out_recv, mode, row)
+
+        def post_row(row):
+            for first in range(lead):
+
+                @pl.when(jnp.logical_and(row == 0, jnp.logical_or(r != 0, m != first)))
+                def _():
+                    post(row, first)
+
             def to(j, carry):
                 mode = lax.rem(m + j, tiles)
-                send(leaving.at[k, mode * strips + row], out_ref.at[me, k], out_send, out_recv,
-                     mode, row)
+
+                @pl.when(jnp.logical_and(
+                    jnp.logical_or(row != r, mode != m), jnp.logical_or(row != 0, mode >= lead)
+                ))
+                def _():
+                    post(row, mode)
+
                 return carry
 
-            return to
-
-        for j in range(strips):
-            row = lax.rem(r + strips // 2 + j, strips)
-            lax.fori_loop(1 if j == strips - strips // 2 else 0, tiles, post(row), 0)
+            lax.fori_loop(0, tiles, to, 0)
+
+        for i in range(half):
+            post_row(opposite(half - 1 - i))
+        for i in range(1, half):
+            post_row(sibling(i))
+        post_row(r)
         pltpu.make_async_copy(leaving.at[k, me], out_ref.at[me, k], out_recv).start()
         return carry
 
-    pl.semaphore_wait(known, tiles - 1)
     lax.fori_loop(0, kept, one_mode, 0)
 
     for q in range(strips):
@@ -400,7 +544,7 @@
     tall = SUB * (strips + 2)
     hbm = pl.BlockSpec(memory_space=pltpu.HBM)
     operands = (order, base.reshape(steps * fields, rows, LANES), land, tangents)
-    dma = pltpu.SemaphoreType.DMA
+    dma, regular = pltpu.SemaphoreType.DMA, pltpu.SemaphoreType.REGULAR
     return pl.pallas_call(
         functools.partial(steps_kernel, strips, tiles, steps, kept),
         out_shape=jax.ShapeDtypeStruct((everyone, kept, fields, rows, LANES), jnp.float32),
@@ -417,7 +561,8 @@
             pltpu.VMEM((tiles, tall, LANES), jnp.float32),
             pltpu.VMEM((2, tiles, tall, LANES), jnp.float32),
             dma((2, strips)), dma((strips,)), dma, dma((tiles,)), dma, dma,
-            dma, dma((kept,)), dma, dma, pltpu.SemaphoreType.REGULAR,
+            dma, dma((kept,)), dma, dma,
+            regular, regular, regular, regular,
             pltpu.VMEM((rows, LANES), jnp.int32), pltpu.SMEM((steps,), jnp.int32), dma((3,)),
         ],
         compiler_params=pltpu.CompilerParams(
@@ -489,7 +634,7 @@
     strips = lax.axis_size("rows")
     held, _, rows, columns = tangents.shape
     fits = (
-        held % strips == 0 and strips > 1 and lax.axis_size("mode") % 2 == 0
+        held % strips == 0 and strips % 2 == 0 and lax.axis_size("mode") % 2 == 0
         and lax.axis_size("mode") > 2 and rows == SUB and checkpoints.shape[-1] == LANES and strips <= 8
         and coefficients.shape[0] % LANES == 0
     )

time: 80.8 us -> 79.4 us (0.983)
  Pallas kernels: 80.6 us -> 79.3 us
    pallas_call x1, Pallas kernels: 79 us -> 77.7 us  [step_modes(): pl.pallas_call(functools.partial(steps_kernel, strips, tiles, steps, kept...]
where the time goes in v1:
time: 79.4 us; the launch traced here: 79.3 us
  Pallas kernels  79.3 us (100%)
    pallas_call x1, Pallas kernels, step_modes(): pl.pallas_call(functools.partial(steps_kernel, strips, tiles, steps, kept...  77.7 us
    pallas_call x1, Pallas kernels, mix(): pl.pallas_call(mix_kernel, out_shape=jax.ShapeDtypeStruct(cells.shape, jn...  1.6 us

profile of v1, /device:TPU:0, one launch (start us, length us, event | category | flops | bytes accessed | tf_op | source)
XLA Modules:
  0.0 79.3 jit_solution(12885157418595657054)
XLA Ops:
  0.0 0.0 copy-start
  0.0 77.7 %shard_map.55 = f32[32,4,3,8,128]{4,3,2,1,0:T(8,128)S(1)} custom-call(s32[8]{0:T(128)} %order_ref.1, f32[24,8,128]{2,1,0:T(8,128)} %bitcast.4, s32[8,1024]{1,0:T(8,128)} %land_ref.1, f32[16,3,8,1024]{3,2,1,0:T(8,128)} %tan_ref.1), custom_call_target="tpu_custom_call" | custom-call | tf_op jit(solution)/shard_map/pallas_call | solution.py:548
  77.7 0.0 copy-done
  77.7 1.6 %shard_map.56 = f32[128,24,128]{2,1,0:T(8,128)} custom-call(f32[128,128]{1,0:T(8,128)S(1)} %copy-done, f32[128,24,128]{2,1,0:T(8,128)S(1)} %bitcast.3), custom_call_target="tpu_custom_call" | custom-call | tf_op jit(solution)/shard_map/pallas_call | solution.py:613
Async XLA Ops:
  0.0 77.7 %copy-start = (f32[128,128]{1,0:T(8,128)S(1)}, f32[128,128]{1,0:T(8,128)}, u32[]{:S(2)}) copy-start(f32[128,128]{1,0:T(8,128)} %coef_ref.1) | copy-start | bytes 196612

commit v2 on v1

--- a/solution.py
+++ b/solution.py
@@ -260,6 +260,20 @@
             device_id=(mode, row), device_id_type=pl.DeviceIdType.MESH,
         ).start()
 
+    def beside(step):
+        chip, target, bit = m // 2, 0, 1
+        if chips & (chips - 1):
+            return lax.rem(chip + step, chips)
+        while bit < chips:
+            target = target + bit * ((chip // bit + step // bit) % 2)
+            bit = 2 * bit
+        return target
+
+    farthest_first = []
+    for step in reversed(range(chips)):
+        chip_there = beside(step)
+        farthest_first += [2 * chip_there + 1 - core, 2 * chip_there + core]
+
     def drain(ref, sem):
         pltpu.make_async_copy(ref, ref, sem).wait()
 
@@ -338,9 +352,60 @@
         for j in range(1, chips):
             send(strip, strip, x_send, x_recv.at[m], other_chip(j), r)
 
-    early = min(2, kept)
-    lead = 2
-    send_in(0, inner)
+    def relay(q):
+
+        @pl.when(jnp.logical_and(q < r, r < strips - 1))
+        def _():
+            pass_up(q)
+
+        @pl.when(jnp.logical_and(q > r, r > 0))
+        def _():
+            pass_down(q)
+
+        spread(q)
+
+    def take_below(j):
+
+        @pl.when(r >= j)
+        def _():
+            drain(base_all.at[m, r - j], z_recv.at[r - j])
+            relay(r - j)
+
+    def take_above(j):
+
+        @pl.when(r + j < strips)
+        def _():
+            drain(base_all.at[m, r + j], z_recv.at[r + j])
+            relay(r + j)
+
+    def hop(j):
+        @pl.when(upper)
+        def _():
+            take_above(j)
+
+        take_below(j)
+
+        @pl.when(jnp.logical_not(upper))
+        def _():
+            take_above(j)
+
+    def send_near(k):
+        send_in(k, opposite(0))
+
+    def send_far(k):
+        for i in range(1, half):
+            send_in(k, opposite(i))
+
+    def send_half(k):
+        for i in range(1, half):
+            send_in(k, sibling(i))
+
+    modes = range(kept)
+
+    @pl.when(at_mid)
+    def _():
+        send_near(0)
+
     fetch_land.wait()
     own[mask_at] = land[...].astype(jnp.float32)
     fetch_base.wait()
@@ -354,9 +419,6 @@
     def _():
         pass_up(r)
 
-    for k in range(1, early):
-        send_in(k, inner)
-
     @pl.when(not_mid)
     def _():
         signal(line, m, inner)
@@ -378,7 +440,10 @@
         def _():
             pass_down(r)
 
-        send_in(0, outer)
+    @pl.when(at_mid)
+    def _():
+        for k in modes[1:2]:
+            send_near(k)
 
     @pl.when(at_end)
     def _():
@@ -394,68 +459,45 @@
     @pl.when(at_mid)
     def _():
         signal(cross, m, inner)
+
+    hop(1)
+    send_half(0)
+
+    @pl.when(at_mid)
+    def _():
         pl.semaphore_wait(cross, 1)
         for i in range(1, half):
             signal(cross, m, sibling(i))
-
-    def send_rest(k):
-        for i in range(half):
-            q = opposite(i)
-            if k < early:
-
-                @pl.when(q != inner)
-                def _():
-                    send_in(k, q)
-            else:
-                send_in(k, q)
-        for i in range(1, half):
-            q = sibling(i)
-            if k < early:
-                done = q == inner
-                if k == 0:
-                    done = jnp.logical_or(done, q == outer)
-
-                @pl.when(jnp.logical_not(done))
-                def _():
-                    send_in(k, q)
-            else:
-                send_in(k, q)
-
-    def relay(q):
-
-        @pl.when(jnp.logical_and(q < r, r < strips - 1))
-        def _():
-            pass_up(q)
-
-        @pl.when(jnp.logical_and(q > r, r > 0))
-        def _():
-            pass_down(q)
-
-        spread(q)
-
-    for j in range(1, strips):
-
-        @pl.when(r >= j)
-        def _():
-            drain(base_all.at[m, r - j], z_recv.at[r - j])
-            relay(r - j)
-
-        @pl.when(r + j < strips)
-        def _():
-            drain(base_all.at[m, r + j], z_recv.at[r + j])
-            relay(r + j)
-
-        if j == 1:
-
-            @pl.when(not_mid)
-            def _():
-                pl.semaphore_wait(cross, 1)
-
-            send_rest(0)
+        for k in modes[2:]:
+            send_near(k)
+
+    for j in range(2, strips):
+        hop(j)
+
+    @pl.when(not_mid)
+    def _():
+        pl.semaphore_wait(cross, 1)
+
+    def send_rest(far, near, beside):
+        for k in far:
+            send_far(k)
+
+        @pl.when(not_mid)
+        def _():
+            for k in near:
+                send_near(k)
+
+        for k in beside:
+            send_half(k)
+
+    send_rest(modes[:1], modes[:2], modes[1:2])
+
+    @pl.when(at_mid)
+    def _():
+        for k in modes[1:2]:
+            send_far(k)
 
     for k in range(kept):
-        if k > 0:
-            send_rest(k)
         pltpu.make_async_copy(tan_ref.at[r * kept + k], whole.at[k, r], in_recv.at[k]).start()
     send(base_all.at[m], base_all.at[m], p_send, p_recv, partner, r)
     for ref in (state, middle, flux):
@@ -464,7 +506,14 @@
         tile = other_chip(j)
         drain(base_all.at[tile], x_recv.at[tile])
         send(base_all.at[tile], base_all.at[tile], p_send, p_recv, partner, r)
+    @pl.when(not_mid)
+    def _():
+        for k in modes[1:2]:
+            send_far(k)
+
+    send_rest((), modes[2:3], modes[2:3])
     drain(base_all.at[pl.ds(0, chips)], p_recv)
+    send_rest(modes[2:], modes[3:], modes[3:])
 
     for strip in range(strips):
         wet[:, pl.ds(SUB * strip, SUB), :] = base_all[:, strip, mask_at]
@@ -485,36 +534,33 @@
                 for t in range(tiles):
                     leaving[k, t * strips + strip, f] = scale * state[f, t, band(strip), :]
 
-        def post(row, mode):
-            send(leaving.at[k, mode * strips + row], out_ref.at[me, k], out_send, out_recv, mode, row)
-
-        def post_row(row):
-            for first in range(lead):
-
-                @pl.when(jnp.logical_and(row == 0, jnp.logical_or(r != 0, m != first)))
-                def _():
-                    post(row, first)
-
-            def to(j, carry):
-                mode = lax.rem(m + j, tiles)
-
-                @pl.when(jnp.logical_and(
-                    jnp.logical_or(row != r, mode != m), jnp.logical_or(row != 0, mode >= lead)
-                ))
-                def _():
-                    post(row, mode)
-
-                return carry
-
-            lax.fori_loop(0, tiles, to, 0)
-
         for i in range(half):
-            post_row(opposite(half - 1 - i))
+            post_row(k, opposite(half - 1 - i))
         for i in range(1, half):
-            post_row(sibling(i))
-        post_row(r)
+            post_row(k, sibling(i))
+        post_row(k, r)
         pltpu.make_async_copy(leaving.at[k, me], out_ref.at[me, k], out_recv).start()
         return carry
+
+    def post_row(k, row):
+        def to(mode):
+            send(leaving.at[k, mode * strips + row], out_ref.at[me, k], out_send, out_recv,
+                 mode, row)
+
+        for lead in (0, 1):
+
+            @pl.when(jnp.logical_and(row == 0, jnp.logical_or(row != r, m != lead)))
+            def _():
+                to(lead)
+
+        for mode in farthest_first:
+            skip = jnp.logical_or(
+                jnp.logical_and(row == r, mode == m), jnp.logical_and(row == 0, mode < 2)
+            )
+
+            @pl.when(jnp.logical_not(skip))
+            def _():
+                to(mode)
 
     lax.fori_loop(0, kept, one_mode, 0)
 

time: 79.4 us -> 78.1 us (0.984)
  Pallas kernels: 79.3 us -> 78 us
    pallas_call x1, Pallas kernels: 77.7 us -> 76.4 us  [step_modes(): pl.pallas_call(functools.partial(steps_kernel, strips, tiles, steps, kept...]
where the time goes in v2:
time: 78.1 us; the launch traced here: 78 us
  Pallas kernels  78 us (100%)
    pallas_call x1, Pallas kernels, step_modes(): pl.pallas_call(functools.partial(steps_kernel, strips, tiles, steps, kept...  76.4 us
    pallas_call x1, Pallas kernels, mix(): pl.pallas_call(mix_kernel, out_shape=jax.ShapeDtypeStruct(cells.shape, jn...  1.6 us

profile of v2, /device:TPU:0, one launch (start us, length us, event | category | flops | bytes accessed | tf_op | source)
XLA Modules:
  0.0 78.0 jit_solution(8794621657374791096)
XLA Ops:
  0.0 0.0 copy-start
  0.0 76.4 %shard_map.55 = f32[32,4,3,8,128]{4,3,2,1,0:T(8,128)S(1)} custom-call(s32[8]{0:T(128)} %order_ref.1, f32[24,8,128]{2,1,0:T(8,128)} %bitcast.4, s32[8,1024]{1,0:T(8,128)} %land_ref.1, f32[16,3,8,1024]{3,2,1,0:T(8,128)} %tan_ref.1), custom_call_target="tpu_custom_call" | custom-call | tf_op jit(solution)/shard_map/pallas_call | solution.py:594
  76.4 0.0 copy-done
  76.4 1.6 %shard_map.56 = f32[128,24,128]{2,1,0:T(8,128)} custom-call(f32[128,128]{1,0:T(8,128)S(1)} %copy-done, f32[128,24,128]{2,1,0:T(8,128)S(1)} %bitcast.3), custom_call_target="tpu_custom_call" | custom-call | tf_op jit(solution)/shard_map/pallas_call | solution.py:659
Async XLA Ops:
  0.0 76.4 %copy-start = (f32[128,128]{1,0:T(8,128)S(1)}, f32[128,128]{1,0:T(8,128)}, u32[]{:S(2)}) copy-start(f32[128,128]{1,0:T(8,128)} %coef_ref.1) | copy-start | bytes 196612

commit v3 on v2

--- a/solution.py
+++ b/solution.py
@@ -235,8 +235,42 @@
     lax.fori_loop(0, steps, one, 0)
 
 
-def steps_kernel(strips, tiles, steps, kept, order_ref, base_ref, land_ref, tan_ref, out_ref,
-                 base_all, whole, leaving, coef, wet, state, middle, flux, flow_pad,
+def halves(values):
+    high = values.astype(jnp.bfloat16)
+    return high, (values - high.astype(jnp.float32)).astype(jnp.bfloat16)
+
+
+def turned_mixing(coefficients):
+    modes = coefficients.shape[0]
+    row = lax.broadcasted_iota(jnp.int32, (modes, modes), 0)
+    col = lax.broadcasted_iota(jnp.int32, (modes, modes), 1)
+    mixing = jnp.where(row <= col, coefficients, 0.0) + jnp.where(row == col, 1.0, 0.0)
+    high, low = halves(mixing.T)
+    return jnp.concatenate(
+        [jnp.concatenate([high, high], 1), jnp.concatenate([low, low], 1)], 0
+    )
+
+
+def mix_rows(turned_ref, cells_ref, group, out_ref):
+    modes, spots, _ = cells_ref.shape
+    cells = cells_ref.reshape(modes * spots, LANES)
+    out = out_ref.reshape(modes * SUB, LANES)
+    turned = turned_ref[...]
+    for spot in range(0, SUB, 2):
+        first = SUB * group + spot
+        high, low = halves(jnp.concatenate(
+            [cells[pl.ds(first + i, modes, stride=spots), :] for i in (0, 1)], 1
+        ))
+        mixed = jnp.dot(
+            turned, jnp.concatenate([high, low], 0), preferred_element_type=jnp.float32
+        )
+        mixed = mixed[:modes] + mixed[modes:]
+        for i in (0, 1):
+            out[pl.ds(spot + i, modes, stride=SUB), :] = mixed[:, LANES * i:LANES * (i + 1)]
+
+
+def steps_kernel(strips, tiles, steps, kept, order_ref, base_ref, land_ref, tan_ref, mix_ref,
+                 turned_ref, out_ref, base_all, whole, mixing, leaving, coef, wet, state, middle, flux, flow_pad,
                  z_send, z_recv, x_send, x_recv, p_send, p_recv,
                  in_send, in_recv, out_send, out_recv, line, plane, half_in, cross,
                  land, order, fetch):
@@ -318,9 +352,11 @@
     fetch_base = pltpu.make_async_copy(base_ref, own.at[pl.ds(0, mask_at)], fetch.at[0])
     fetch_land = pltpu.make_async_copy(tile_of_land, land, fetch.at[1])
     fetch_order = pltpu.make_async_copy(order_ref, order, fetch.at[2])
+    fetch_mixing = pltpu.make_async_copy(mix_ref, mixing, fetch.at[3])
     fetch_land.start()
     fetch_base.start()
     fetch_order.start()
+    fetch_mixing.start()
 
     @pl.when(at_end)
     def _():
@@ -473,10 +509,12 @@
 
     for j in range(2, strips):
         hop(j)
-
-    @pl.when(not_mid)
-    def _():
-        pl.semaphore_wait(cross, 1)
+        if j == 2:
+
+            @pl.when(not_mid)
+            def _():
+                pl.semaphore_wait(cross, 1)
+                send_near(0)
 
     def send_rest(far, near, beside):
         for k in far:
@@ -490,7 +528,7 @@
         for k in beside:
             send_half(k)
 
-    send_rest(modes[:1], modes[:2], modes[1:2])
+    send_rest(modes[:1], modes[1:2], modes[1:2])
 
     @pl.when(at_mid)
     def _():
@@ -534,36 +572,37 @@
                 for t in range(tiles):
                     leaving[k, t * strips + strip, f] = scale * state[f, t, band(strip), :]
 
+        def post_row(row):
+            def to(mode):
+                send(leaving.at[k, mode * strips + row], out_ref.at[me, k], out_send, out_recv,
+                     mode, row)
+
+            for lead in (0, 1):
+
+                @pl.when(jnp.logical_and(row == 0, jnp.logical_or(row != r, m != lead)))
+                def _():
+                    to(lead)
+
+            for mode in farthest_first:
+                skip = jnp.logical_or(
+                    jnp.logical_and(row == r, mode == m), jnp.logical_and(row == 0, mode < 2)
+                )
+
+                @pl.when(jnp.logical_not(skip))
+                def _():
+                    to(mode)
+
         for i in range(half):
-            post_row(k, opposite(half - 1 - i))
+            post_row(opposite(half - 1 - i))
         for i in range(1, half):
-            post_row(k, sibling(i))
-        post_row(k, r)
+            post_row(sibling(i))
+        post_row(r)
         pltpu.make_async_copy(leaving.at[k, me], out_ref.at[me, k], out_recv).start()
         return carry
 
-    def post_row(k, row):
-        def to(mode):
-            send(leaving.at[k, mode * strips + row], out_ref.at[me, k], out_send, out_recv,
-                 mode, row)
-
-        for lead in (0, 1):
-
-            @pl.when(jnp.logical_and(row == 0, jnp.logical_or(row != r, m != lead)))
-            def _():
-                to(lead)
-
-        for mode in farthest_first:
-            skip = jnp.logical_or(
-                jnp.logical_and(row == r, mode == m), jnp.logical_and(row == 0, mode < 2)
-            )
-
-            @pl.when(jnp.logical_not(skip))
-            def _():
-                to(mode)
-
     lax.fori_loop(0, kept, one_mode, 0)
-
+    fetch_mixing.wait()
+    turned_ref[...] = turned_mixing(mixing[...])
     for q in range(strips):
 
         @pl.when(jnp.logical_and(q <= r, r < strips - 1))
@@ -581,24 +620,29 @@
     drain(out_ref, out_recv)
 
 
-def step_modes(order, base, land, tangents):
+def step_modes(order, base, land, tangents, coefficients):
     strips, tiles = lax.axis_size("rows"), lax.axis_size("mode")
     held, fields, rows, columns = tangents.shape
     steps = base.shape[0]
     kept = held // strips
     everyone = tiles * strips
+    modes = everyone * kept
     tall = SUB * (strips + 2)
-    hbm = pl.BlockSpec(memory_space=pltpu.HBM)
-    operands = (order, base.reshape(steps * fields, rows, LANES), land, tangents)
+    hbm, vmem = (pl.BlockSpec(memory_space=space) for space in (pltpu.HBM, pltpu.VMEM))
+    operands = (order, base.reshape(steps * fields, rows, LANES), land, tangents, coefficients)
     dma, regular = pltpu.SemaphoreType.DMA, pltpu.SemaphoreType.REGULAR
     return pl.pallas_call(
         functools.partial(steps_kernel, strips, tiles, steps, kept),
-        out_shape=jax.ShapeDtypeStruct((everyone, kept, fields, rows, LANES), jnp.float32),
-        in_specs=[hbm] * 4,
-        out_specs=pl.BlockSpec(memory_space=pl.ANY),
+        out_shape=(
+            jax.ShapeDtypeStruct((2 * modes, 2 * modes), jnp.bfloat16),
+            jax.ShapeDtypeStruct((everyone, kept, fields, rows, LANES), jnp.float32),
+        ),
+        in_specs=[hbm] * 5,
+        out_specs=(vmem, pl.BlockSpec(memory_space=pl.ANY)),
         scratch_shapes=[
             pltpu.VMEM((tiles, strips, steps * fields + 1, rows, LANES), jnp.float32),
             pltpu.VMEM((kept, strips, fields, rows, columns), jnp.float32),
+            pltpu.VMEM((modes, modes), jnp.float32),
             pltpu.VMEM((kept, everyone, fields, rows, LANES), jnp.float32),
             pltpu.VMEM((steps, COEFS, tiles, SUB * strips, LANES), jnp.float32),
             pltpu.VMEM((tiles, SUB * strips, LANES), jnp.float32),
@@ -609,43 +653,18 @@
             dma((2, strips)), dma((strips,)), dma, dma((tiles,)), dma, dma,
             dma, dma((kept,)), dma, dma,
             regular, regular, regular, regular,
-            pltpu.VMEM((rows, LANES), jnp.int32), pltpu.SMEM((steps,), jnp.int32), dma((3,)),
+            pltpu.VMEM((rows, LANES), jnp.int32), pltpu.SMEM((steps,), jnp.int32), dma((4,)),
         ],
         compiler_params=pltpu.CompilerParams(
-            collective_id=0, has_side_effects=True, vmem_limit_bytes=24 << 20
+            collective_id=0, has_side_effects=True, vmem_limit_bytes=32 << 20
         ),
     )(*(pltpu.with_memory_space_constraint(held_in_hbm, pltpu.HBM) for held_in_hbm in operands))
 
 
-def halves(values):
-    high = values.astype(jnp.bfloat16)
-    return high, (values - high.astype(jnp.float32)).astype(jnp.bfloat16)
-
-
-def mix_kernel(coef_ref, cells_ref, out_ref, staged, sems):
-    modes, spots, _ = cells_ref.shape
-    row = lax.broadcasted_iota(jnp.int32, (modes, modes), 0)
-    col = lax.broadcasted_iota(jnp.int32, (modes, modes), 1)
-    mixing = jnp.where(row <= col, coef_ref[...], 0.0) + jnp.where(row == col, 1.0, 0.0)
-    high, low = halves(mixing.T)
-    turned = jnp.concatenate(
-        [jnp.concatenate([high, high], 1), jnp.concatenate([low, low], 1)], 0
-    )
-    cells = cells_ref.reshape(modes * spots, LANES)
+def mix_kernel(turned_ref, cells_ref, out_ref, staged, sems):
     copies = []
-    for group in range(spots // SUB):
-        out = staged.at[group].reshape(modes * SUB, LANES)
-        for spot in range(0, SUB, 2):
-            first = SUB * group + spot
-            high, low = halves(jnp.concatenate(
-                [cells[pl.ds(first + i, modes, stride=spots), :] for i in (0, 1)], 1
-            ))
-            mixed = jnp.dot(
-                turned, jnp.concatenate([high, low], 0), preferred_element_type=jnp.float32
-            )
-            mixed = mixed[:modes] + mixed[modes:]
-            for i in (0, 1):
-                out[pl.ds(spot + i, modes, stride=SUB), :] = mixed[:, LANES * i:LANES * (i + 1)]
+    for group in range(staged.shape[0]):
+        mix_rows(turned_ref, cells_ref, group, staged.at[group])
         copies.append(pltpu.make_async_copy(
             staged.at[group], out_ref.at[:, pl.ds(SUB * group, SUB)], sems.at[group]
         ))
@@ -654,7 +673,7 @@
         copy.wait()
 
 
-def mix(coefficients, cells):
+def mix(turned, cells):
     modes, spots, _ = cells.shape
     return pl.pallas_call(
         mix_kernel,
@@ -666,14 +685,14 @@
             pltpu.SemaphoreType.DMA((spots // SUB,)),
         ],
         compiler_params=pltpu.CompilerParams(vmem_limit_bytes=8 << 20),
-    )(coefficients, cells)
+    )(turned, cells)
 
 
 def on_device_whole(tangents, checkpoints, owner_order, land_mask, coefficients):
     fields, rows = tangents.shape[1:3]
-    placed = step_modes(owner_order, checkpoints, land_mask, tangents)
-    mixed = mix(coefficients, placed.reshape(coefficients.shape[0], fields * rows, LANES))
-    return mixed.reshape(coefficients.shape[0], fields, rows, LANES)
+    turned, placed = step_modes(owner_order, checkpoints, land_mask, tangents, coefficients)
+    whole = mix(turned, placed.reshape(-1, fields * rows, LANES))
+    return whole.reshape(-1, fields, rows, LANES)
 
 
 def on_device(tangents, checkpoints, owner_order, land_mask, coefficients):
@@ -682,6 +701,7 @@
     fits = (
         held % strips == 0 and strips % 2 == 0 and lax.axis_size("mode") % 2 == 0
         and lax.axis_size("mode") > 2 and rows == SUB and checkpoints.shape[-1] == LANES and strips <= 8
+        and coefficients.shape[0] == held * lax.axis_size("mode")
         and coefficients.shape[0] % LANES == 0
     )
     chosen = on_device_whole if fits else on_device_general

time: 78.1 us -> 77.6 us (level)
  Pallas kernels: 78 us -> 76.9 us
    pallas_call x1, Pallas kernels: 76.4 us -> 75.4 us  [step_modes(): pl.pallas_call(functools.partial(steps_kernel, strips, tiles, steps, kept...]
where the time goes in v3:
time: 77.6 us; the launch traced here: 76.9 us
  Pallas kernels  76.9 us (99%)
    pallas_call x1, Pallas kernels, step_modes(): pl.pallas_call(functools.partial(steps_kernel, strips, tiles, steps, kept...  75.4 us

profile of v3, /device:TPU:0, one launch (start us, length us, event | category | flops | bytes accessed | tf_op | source)
XLA Modules:
  0.0 76.9 jit_solution(16807472667790965056)
XLA Ops:
  0.0 75.4 %shard_map.55 = (bf16[256,256]{1,0:T(8,128)(2,1)S(1)}, f32[32,4,3,8,128]{4,3,2,1,0:T(8,128)S(1)}) custom-call(s32[8]{0:T(128)} %order_ref.1, f32[24,8,128]{2,1,0:T(8,128)} %bitcast.4, s32[8,1024]{1,0:T(8,128)} %land_ref.1, f32[16,3,8,1024]{3,2,1,0:T(8,128)} %tan_ref.1, f32[128,128]{1,0:T(8,128)} %mix_ref.1), custom_call_target="tpu_custom_call" | custom-call | tf_op jit(solution)/shard_map/pallas_call | solution.py:634
  75.4 1.6 %shard_map.56 = f32[128,24,128]{2,1,0:T(8,128)} custom-call(bf16[256,256]{1,0:T(8,128)(2,1)S(1)} %get-tuple-element.7.turned_ref, f32[128,24,128]{2,1,0:T(8,128)S(1)} %bitcast.3), custom_call_target="tpu_custom_call" | custom-call | tf_op jit(solution)/shard_map/pallas_call | solution.py:678

commit v4 on v3

--- a/solution.py
+++ b/solution.py
@@ -240,15 +240,23 @@
     return high, (values - high.astype(jnp.float32)).astype(jnp.bfloat16)
 
 
-def turned_mixing(coefficients):
+def full_mixing(coefficients):
     modes = coefficients.shape[0]
     row = lax.broadcasted_iota(jnp.int32, (modes, modes), 0)
     col = lax.broadcasted_iota(jnp.int32, (modes, modes), 1)
-    mixing = jnp.where(row <= col, coefficients, 0.0) + jnp.where(row == col, 1.0, 0.0)
+    return jnp.where(row <= col, coefficients, 0.0) + jnp.where(row == col, 1.0, 0.0)
+
+
+def turned_mixing(mixing):
     high, low = halves(mixing.T)
     return jnp.concatenate(
         [jnp.concatenate([high, high], 1), jnp.concatenate([low, low], 1)], 0
     )
+
+
+def turned_few(mixing):
+    high, low = halves(mixing.T)
+    return jnp.concatenate([high, high, low, low], 1)
 
 
 def mix_rows(turned_ref, cells_ref, group, out_ref):
@@ -270,9 +278,9 @@
 
 
 def steps_kernel(strips, tiles, steps, kept, order_ref, base_ref, land_ref, tan_ref, mix_ref,
-                 turned_ref, out_ref, base_all, whole, mixing, leaving, coef, wet, state, middle, flux, flow_pad,
+                 few_ref, partial_ref, late_ref, cells, base_all, whole, mixing, turned, leaving, coef, wet, state, middle, flux, flow_pad,
                  z_send, z_recv, x_send, x_recv, p_send, p_recv,
-                 in_send, in_recv, out_send, out_recv, line, plane, half_in, cross,
+                 in_send, in_recv, out_send, out_recv, late_recv, line, plane, half_in, cross,
                  land, order, fetch):
     m = lax.axis_index("mode")
     r = lax.axis_index("rows")
@@ -557,7 +565,10 @@
         wet[:, pl.ds(SUB * strip, SUB), :] = base_all[:, strip, mask_at]
     build_coefs(order, base_all, coef, flow_pad, strips, steps, lane)
 
-    def one_mode(k, carry):
+    final = kept - 1
+    slot = lax.rem(r, half) * tiles + m
+
+    def one_mode(k, carry, last=False):
         drain(whole.at[k], in_recv.at[k])
         for f, scale in enumerate((0.25, 1.0, 1.0)):
             for strip in range(strips):
@@ -572,10 +583,12 @@
                 for t in range(tiles):
                     leaving[k, t * strips + strip, f] = scale * state[f, t, band(strip), :]
 
-        def post_row(row):
+        def post_row(row, late=False):
             def to(mode):
-                send(leaving.at[k, mode * strips + row], out_ref.at[me, k], out_send, out_recv,
-                     mode, row)
+                target, received = (
+                    (late_ref.at[slot], late_recv) if late else (cells.at[me, k], out_recv)
+                )
+                send(leaving.at[k, mode * strips + row], target, out_send, received, mode, row)
 
             for lead in (0, 1):
 
@@ -593,16 +606,37 @@
                     to(mode)
 
         for i in range(half):
-            post_row(opposite(half - 1 - i))
+            post_row(opposite(half - 1 - i), last)
         for i in range(1, half):
             post_row(sibling(i))
         post_row(r)
-        pltpu.make_async_copy(leaving.at[k, me], out_ref.at[me, k], out_recv).start()
+        pltpu.make_async_copy(leaving.at[k, me], cells.at[me, k], out_recv).start()
         return carry
 
-    lax.fori_loop(0, kept, one_mode, 0)
+    lax.fori_loop(0, final, one_mode, 0)
+    one_mode(final, 0, last=True)
+
+    there = jnp.where(upper, 0, half)
     fetch_mixing.wait()
-    turned_ref[...] = turned_mixing(mixing[...])
+    mixing[...] = full_mixing(mixing[...])
+    turned[...] = turned_mixing(mixing[...])
+    pace = strips * kept
+
+    def few_rows(first):
+        return jnp.concatenate(
+            [mixing[pl.ds((first + i) * kept + final, tiles, stride=pace), :] for i in range(half)], 0
+        )
+
+    few_ref[...] = turned_few(jnp.where(upper, few_rows(0), few_rows(half)))
+    for mode in range(tiles):
+        for i in range(half):
+            cells[mode * strips + there + i, final] = jnp.zeros(cells.shape[2:], jnp.float32)
+    early = everyone * final + everyone // 2
+    drain(cells.reshape((everyone * kept,) + cells.shape[2:]).at[pl.ds(0, early)], out_recv)
+    spots = cells.shape[2] * SUB
+    for group in range(cells.shape[2]):
+        mix_rows(turned, cells.reshape(everyone * kept, spots, LANES), group, partial_ref.at[group])
+
     for q in range(strips):
 
         @pl.when(jnp.logical_and(q <= r, r < strips - 1))
@@ -617,7 +651,7 @@
     drain(base_all.at[pl.ds(0, chips)], p_send)
     drain(whole.at[:, pl.ds(0, strips - 1)], in_send)
     drain(leaving.at[:, pl.ds(0, everyone - 1)], out_send)
-    drain(out_ref, out_recv)
+    drain(late_ref, late_recv)
 
 
 def step_modes(order, base, land, tangents, coefficients):
@@ -626,7 +660,7 @@
     steps = base.shape[0]
     kept = held // strips
     everyone = tiles * strips
-    modes = everyone * kept
+    modes, late = everyone * kept, everyone // 2
     tall = SUB * (strips + 2)
     hbm, vmem = (pl.BlockSpec(memory_space=space) for space in (pltpu.HBM, pltpu.VMEM))
     operands = (order, base.reshape(steps * fields, rows, LANES), land, tangents, coefficients)
@@ -634,15 +668,18 @@
     return pl.pallas_call(
         functools.partial(steps_kernel, strips, tiles, steps, kept),
         out_shape=(
-            jax.ShapeDtypeStruct((2 * modes, 2 * modes), jnp.bfloat16),
-            jax.ShapeDtypeStruct((everyone, kept, fields, rows, LANES), jnp.float32),
+            jax.ShapeDtypeStruct((modes, 4 * late), jnp.bfloat16),
+            jax.ShapeDtypeStruct((fields, modes, rows, LANES), jnp.float32),
+            jax.ShapeDtypeStruct((late, fields, rows, LANES), jnp.float32),
         ),
         in_specs=[hbm] * 5,
-        out_specs=(vmem, pl.BlockSpec(memory_space=pl.ANY)),
+        out_specs=(vmem, vmem, pl.BlockSpec(memory_space=pl.ANY)),
         scratch_shapes=[
+            pltpu.VMEM((everyone, kept, fields, rows, LANES), jnp.float32),
             pltpu.VMEM((tiles, strips, steps * fields + 1, rows, LANES), jnp.float32),
             pltpu.VMEM((kept, strips, fields, rows, columns), jnp.float32),
             pltpu.VMEM((modes, modes), jnp.float32),
+            pltpu.VMEM((2 * modes, 2 * modes), jnp.bfloat16),
             pltpu.VMEM((kept, everyone, fields, rows, LANES), jnp.float32),
             pltpu.VMEM((steps, COEFS, tiles, SUB * strips, LANES), jnp.float32),
             pltpu.VMEM((tiles, SUB * strips, LANES), jnp.float32),
@@ -651,7 +688,7 @@
             pltpu.VMEM((tiles, tall, LANES), jnp.float32),
             pltpu.VMEM((2, tiles, tall, LANES), jnp.float32),
             dma((2, strips)), dma((strips,)), dma, dma((tiles,)), dma, dma,
-            dma, dma((kept,)), dma, dma,
+            dma, dma((kept,)), dma, dma, dma,
             regular, regular, regular, regular,
             pltpu.VMEM((rows, LANES), jnp.int32), pltpu.SMEM((steps,), jnp.int32), dma((4,)),
         ],
@@ -661,10 +698,26 @@
     )(*(pltpu.with_memory_space_constraint(held_in_hbm, pltpu.HBM) for held_in_hbm in operands))
 
 
-def mix_kernel(turned_ref, cells_ref, out_ref, staged, sems):
+def add_last(few_ref, partial_ref, late_ref, out_ref, staged, sems):
+    late, spots, _ = late_ref.shape
+    groups, modes = partial_ref.shape[:2]
+    cells = late_ref.reshape(late * spots, LANES)
+    few = few_ref[...]
     copies = []
-    for group in range(staged.shape[0]):
-        mix_rows(turned_ref, cells_ref, group, staged.at[group])
+    for group in range(groups):
+        start = partial_ref.at[group].reshape(modes * SUB, LANES)
+        out = staged.at[group].reshape(modes * SUB, LANES)
+        for spot in range(0, SUB, 2):
+            first = SUB * group + spot
+            high, low = halves(jnp.concatenate(
+                [cells[pl.ds(first + i, late, stride=spots), :] for i in (0, 1)], 1
+            ))
+            mixed = jnp.dot(
+                few, jnp.concatenate([high, low, high, low], 0), preferred_element_type=jnp.float32
+            )
+            for i in (0, 1):
+                row = pl.ds(spot + i, modes, stride=SUB)
+                out[row, :] = start[row, :] + mixed[:, LANES * i:LANES * (i + 1)]
         copies.append(pltpu.make_async_copy(
             staged.at[group], out_ref.at[:, pl.ds(SUB * group, SUB)], sems.at[group]
         ))
@@ -673,25 +726,25 @@
         copy.wait()
 
 
-def mix(turned, cells):
-    modes, spots, _ = cells.shape
+def mix(few, partial, late):
+    groups, modes = partial.shape[:2]
     return pl.pallas_call(
-        mix_kernel,
-        out_shape=jax.ShapeDtypeStruct(cells.shape, jnp.float32),
-        in_specs=[pl.BlockSpec(memory_space=pltpu.VMEM)] * 2,
+        add_last,
+        out_shape=jax.ShapeDtypeStruct((modes, groups * SUB, LANES), jnp.float32),
+        in_specs=[pl.BlockSpec(memory_space=pltpu.VMEM)] * 3,
         out_specs=pl.BlockSpec(memory_space=pltpu.HBM),
         scratch_shapes=[
-            pltpu.VMEM((spots // SUB, modes, SUB, LANES), jnp.float32),
-            pltpu.SemaphoreType.DMA((spots // SUB,)),
+            pltpu.VMEM((groups, modes, SUB, LANES), jnp.float32),
+            pltpu.SemaphoreType.DMA((groups,)),
         ],
         compiler_params=pltpu.CompilerParams(vmem_limit_bytes=8 << 20),
-    )(turned, cells)
+    )(few, partial, late)
 
 
 def on_device_whole(tangents, checkpoints, owner_order, land_mask, coefficients):
     fields, rows = tangents.shape[1:3]
-    turned, placed = step_modes(owner_order, checkpoints, land_mask, tangents, coefficients)
-    whole = mix(turned, placed.reshape(-1, fields * rows, LANES))
+    few, partial, late = step_modes(owner_order, checkpoints, land_mask, tangents, coefficients)
+    whole = mix(few, partial, late.reshape(-1, fields * rows, LANES))
     return whole.reshape(-1, fields, rows, LANES)
 
 

time: 77.6 us -> 77.6 us (level)
  no operation moved by 1% of the time
where the time goes in v4:
time: 77.6 us; the launch traced here: 76.9 us
  Pallas kernels  76.9 us (99%)
    pallas_call x1, Pallas kernels, step_modes(): pl.pallas_call(functools.partial(steps_kernel, strips, tiles, steps, kept...  75.4 us

profile of v4, /device:TPU:0, one launch (start us, length us, event | category | flops | bytes accessed | tf_op | source)
XLA Modules:
  0.0 76.9 jit_solution(4831155281182459964)
XLA Ops:
  0.0 75.4 %shard_map.55 = (bf16[128,64]{1,0:T(8,128)(2,1)S(1)}, f32[3,128,8,128]{3,2,1,0:T(8,128)S(1)}, f32[16,3,8,128]{3,2,1,0:T(8,128)S(1)}) custom-call(s32[8]{0:T(128)} %order_ref.1, f32[24,8,128]{2,1,0:T(8,128)} %bitcast.4, s32[8,1024]{1,0:T(8,128)} %land_ref.1, f32[16,3,8,1024]{3,2,1,0:T(8,128)} %tan_ref.1, f32[128,128]{1,0:T(8,128)} %mix_ref.1), custom_call_target="tpu_custom_call" | custom-call | tf_op jit(solution)/shard_map/pallas_call | solution.py:668
  75.4 1.5 %shard_map.56 = f32[128,24,128]{2,1,0:T(8,128)} custom-call(bf16[128,64]{1,0:T(8,128)(2,1)S(1)} %get-tuple-element.8.few_ref, f32[3,128,8,128]{3,2,1,0:T(8,128)S(1)} %get-tuple-element.9.partial_ref, f32[16,24,128]{2,1,0:T(8,128)S(1)} %bitcast.3), custom_call_target="tpu_custom_call" | custom-call | tf_op jit(solution)/shard_map/pallas_call | solution.py:731
